TPU v7x, 32 devices: a whole 2x2x4 slice. The times are simulated.
32 devices in a mesh: band: 4 (over y, core), grid: 8 (over z, x).
Axes of the slice: x: 2, y: 2, z: 4, core: 2. Of those that a mesh axis runs over, the one named last changes fastest.
Arguments:
- orbitals: float32 [64, 16, 4096], P('band', 'grid'), may hold values from -6 to 6
- potential: float32 [16, 4096], P('grid'), may hold values from 0 to 2
Outputs:
- rotated: bfloat16 [64, 16, 4096], P('band', 'grid')
All inputs are finite; a program needn't handle non-finite values. Where the computation divides by a largest or mean magnitude, that divisor is 1e-20 or more.
Results may differ from a plain program's by a relative error of at most 0.001.
The roundings to bfloat16 on the way count: a program that leaves them out, or rounds other values in their place, can miss the bound.
Values may be sent and summed in bfloat16 or wider, within the bound.
A program may use at most 64 MiB of HBM per device.

v0:
```python
import jax
import jax.numpy as jnp
from jax import lax
from jax.sharding import PartitionSpec as P

NX = 64
DEGREE = 2
NS_ITERS = 2


def with_halo(block, sides, width):
    for axis, dim in sides:
        count = lax.axis_size(axis)
        forward = [(i, i + 1) for i in range(count - 1)]
        forward.append((count - 1, 0))
        backward = [(target, source) for source, target in forward]
        low = lax.ppermute(
            lax.slice_in_dim(block, block.shape[dim] - width, None, axis=dim), axis, forward
        )
        high = lax.ppermute(lax.slice_in_dim(block, 0, width, axis=dim), axis, backward)
        block = jnp.concatenate([low, block, high], axis=dim)
    return block


def apply_inner(extended, potential):
    inner = extended[:, 1:-1]
    count = inner.shape[0]
    planes = inner.shape[1]
    square = inner.reshape(count, planes, NX, NX)
    sideways = jnp.roll(square, 1, 2) + jnp.roll(square, -1, 2)
    sideways = sideways + jnp.roll(square, 1, 3) + jnp.roll(square, -1, 3)
    beside = extended[:, 2:] + extended[:, :-2] + sideways.reshape(inner.shape)
    return 0.5 * (6.0 * inner - beside) + potential[None] * inner


def local(orbitals, potential):
    previous = orbitals
    current = orbitals
    for degree_step in range(DEGREE):
        extended = with_halo(current, (("grid", 1),), 1)
        applied = apply_inner(extended, potential)
        if degree_step == 0:
            following = (applied - 5.0 * current) / 3.0
        else:
            following = 2.0 * (applied - 5.0 * current) / 3.0 - previous
        previous = current
        current = following
    count, zplanes, width = orbitals.shape
    filtered = current.astype(jnp.bfloat16).reshape(count, zplanes * width)
    pieces = lax.all_to_all(filtered, "band", split_axis=1, concat_axis=0, tiled=True)
    total_cells = pieces.shape[1] * lax.axis_size("band") * lax.axis_size("grid")
    partial_value = (
        lax.dot_general(
            pieces, pieces, (((1,), (1,)), ((), ())), preferred_element_type=jnp.float32
        )
        / total_cells
    )
    gram = lax.psum(partial_value, ("band", "grid"))
    scale = jnp.max(jnp.sum(jnp.abs(gram), axis=1))
    identity_mat = jnp.eye(gram.shape[0], dtype=jnp.float32)
    upper = gram / scale
    lower = identity_mat
    for sweep in range(NS_ITERS):
        factor = 1.5 * identity_mat - 0.5 * jnp.dot(lower, upper, precision=lax.Precision.HIGHEST)
        upper = jnp.dot(upper, factor, precision=lax.Precision.HIGHEST)
        lower = jnp.dot(factor, lower, precision=lax.Precision.HIGHEST)
    root = (lower / jnp.sqrt(scale)).astype(jnp.bfloat16)
    turned = lax.dot_general(
        root, pieces, (((0,), (0,)), ((), ())), preferred_element_type=jnp.float32
    )
    turned = turned.astype(jnp.bfloat16)
    returned = lax.all_to_all(turned, "band", split_axis=0, concat_axis=1, tiled=True)
    return returned.reshape(count, zplanes, width)


def solution(mesh):
    placed = (P("band", "grid", None), P("grid", None))
    return jax.shard_map(
        local, mesh=mesh, in_specs=placed, out_specs=P("band", "grid", None), check_vma=False
    )
```

profile of v0, /device:TPU:0, one launch (start us, length us, event | category | flops | bytes accessed | tf_op | source)
XLA Modules:
  0.0 102.4 jit_solution(3121627851999156750)
XLA Ops:
  0.0 0.0 copy-start
  0.0 1.9 %fusion.24 = (f32[16,1,4096]{2,1,0:T(1,128)S(1)}, f32[16,1,4096]{2,1,0:T(1,128)S(1)}) fusion(f32[16,2,4096]{2,1,0:T(2,128)} %param.2), kind=kLoop, calls=%fused_computation.42 | loop fusion | bytes 1048576 | tf_op jit(solution)/shard_map/slice | solution.py:20
  1.9 6.1 %collective-permute-start = (f32[16,1,4096]{2,1,0:T(1,128)S(1)}, f32[16,1,4096]{2,1,0:T(1,128)S(1)}, u32[]{:S(2)}, u32[]{:S(2)}) collective-permute-start(f32[16,1,4096]{2,1,0:T(1,128)S(1)} %get-tuple-element.25), channel_id=1, source_target_pairs={{1,0},{2,1},{3,2},{4,3},{5,4},{6,5},{7,6},{0,7},{9,8},{10,9},{11,1... | collective-permute-start | bytes 786440 | tf_op jit(solution)/shard_map/ppermute | solution.py:20
  7.9 0.0 collective-permute-start.1
  7.9 0.0 copy-done
  7.9 0.6 reshape.35
  8.6 0.4 fusion.19
  8.9 0.4 fusion.20
  9.3 0.0 copy-start.1
  9.3 0.2 fusion.21
  9.5 0.5 copy-done.1
  10.1 0.9 fusion.4
  11.0 0.5 add.58
  11.5 2.0 %collective-permute-done = f32[16,1,4096]{2,1,0:T(1,128)S(1)} collective-permute-done((f32[16,1,4096]{2,1,0:T(1,128)S(1)}, f32[16,1,4096]{2,1,0:T(1,128)S(1)}, u32[]{:S(2)}, u32[]{:S(2)}) %collective-permute-start) | collective-permute-done | bytes 262176 | tf_op jit(solution)/shard_map/ppermute | solution.py:20
  13.5 5.0 %collective-permute-done.1 = f32[16,1,4096]{2,1,0:T(1,128)} collective-permute-done((f32[16,1,4096]{2,1,0:T(1,128)S(1)}, f32[16,1,4096]{2,1,0:T(1,128)}, u32[]{:S(2)}, u32[]{:S(2)}) %collective-permute-start.1) | collective-permute-done | bytes 262176 | tf_op jit(solution)/shard_map/ppermute | solution.py:17
  18.5 2.4 %broadcast_multiply_fusion = (f32[16,2,4096]{2,1,0:T(2,128)S(1)}, f32[16,2,4096]{2,1,0:T(2,128)S(1)}) fusion(f32[16,2,4096]{2,1,0:T(2,128)S(1)} %copy-done, f32[2,4096]{1,0:T(2,128)S(1)} %copy-done.1, f32[16,2,4096]{2,1,0:T(2,128)S(1)} %add.58, f32[16,1,4096]{2,1,0:T(1,128)} %collective-permute-done.1, f32[16,1,4096]{2,1,0:T(1,128)S(1)} %collective-permute-done), kind=kLoop, calls=%fused_computation.26 | loop fusion | flops 1572864 | bytes 2654208 | tf_op jit(solution)/shard_map/div | solution.py:43
  21.0 0.6 reshape.36
  21.6 0.4 fusion.16
  22.0 0.2 fusion.17
  22.2 0.4 fusion.15
  22.5 1.3 %fusion.23 = (f32[16,1,4096]{2,1,0:T(1,128)}, f32[16,1,4096]{2,1,0:T(1,128)}) fusion(f32[16,2,4096]{2,1,0:T(2,128)S(1)} %get-tuple-element.5), kind=kLoop, calls=%fused_computation.41 | loop fusion | bytes 1048576 | tf_op jit(solution)/shard_map/slice | solution.py:20
  23.9 3.5 %collective-permute-start.2 = (f32[16,1,4096]{2,1,0:T(1,128)}, f32[16,1,4096]{2,1,0:T(1,128)S(1)}, u32[]{:S(2)}, u32[]{:S(2)}) collective-permute-start(f32[16,1,4096]{2,1,0:T(1,128)} %get-tuple-element.23), channel_id=1, source_target_pairs={{1,0},{2,1},{3,2},{4,3},{5,4},{6,5},{7,6},{0,7},{9,8},{10,9},{11,1... | collective-permute-start | bytes 786440 | tf_op jit(solution)/shard_map/ppermute | solution.py:20
  27.3 0.0 collective-permute-start.3
  27.4 0.9 fusion.6
  28.2 0.5 add.65
  28.8 8.5 %collective-permute-done.2 = f32[16,1,4096]{2,1,0:T(1,128)S(1)} collective-permute-done((f32[16,1,4096]{2,1,0:T(1,128)}, f32[16,1,4096]{2,1,0:T(1,128)S(1)}, u32[]{:S(2)}, u32[]{:S(2)}) %collective-permute-start.2) | collective-permute-done | bytes 262176 | tf_op jit(solution)/shard_map/ppermute | solution.py:20
  37.2 0.3 collective-permute-done.3
  37.5 2.6 %subtract_convert_fusion = bf16[16,2,4096]{2,1,0:T(2,128)(2,1)S(1)} fusion(f32[16,2,4096]{2,1,0:T(2,128)S(1)} %copy-done, f32[16,2,4096]{2,1,0:T(2,128)S(1)} %get-tuple-element.6, f32[16,2,4096]{2,1,0:T(2,128)S(1)} %add.65, f32[16,2,4096]{2,1,0:T(2,128)S(1)} %get-tuple-element.5, f32[16,1,4096]{2,1,0:T(1,128)} %collective-permute-done.3, ...), kind=kLoop, calls=%fused_computation.24 | loop fusion | flops 1835008 | bytes 2916352 | tf_op jit(solution)/shard_map/convert_element_type | solution.py:49
  40.1 0.1 all_to_all.26
  40.2 0.2 copy.7
  40.3 8.6 %all_to_all.35 = bf16[16,4,2048]{2,0,1:T(8,128)(2,1)S(1)} all-to-all(bf16[16,4,2048]{2,0,1:T(8,128)(2,1)S(1)} %copy.7), channel_id=1, replica_groups=mesh['band'=4,'grid'=8] {'band'}, dimensions={1} | all-to-all | bytes 524288 | tf_op jit(solution)/shard_map/all_to_all | solution.py:50
  48.9 0.2 convolution_multiply_fusion.2
  49.1 39.0 %psum.7 = f32[64,64]{1,0:T(8,128)S(1)} all-reduce(f32[64,64]{1,0:T(8,128)S(1)} %convolution_multiply_fusion.2), channel_id=1, replica_groups=mesh['band'=4,'grid'=8] {'band','grid'}, use_global_device_ids=true, to_apply=%region_0.1 | all-reduce | flops 4096 | bytes 32768 | tf_op jit(solution)/shard_map/psum | solution.py:58
  88.1 0.1 abs_reduce_fusion
  88.2 0.6 reduce_max.9
  88.8 0.8 fusion.1
  89.6 0.8 fusion.14
  90.4 0.1 fusion.13
  91.3 0.2 fusion
  91.5 0.2 fusion.2
  91.6 0.2 convolution_convert_fusion
  91.9 9.4 %all_to_all.36 = bf16[4,16,2048]{2,1,0:T(8,128)(2,1)S(1)} all-to-all(bf16[4,16,2048]{2,1,0:T(8,128)(2,1)S(1)} %bitcast.21), channel_id=1, replica_groups=mesh['band'=4,'grid'=8] {'band'}, dimensions={0} | all-to-all | bytes 524288 | tf_op jit(solution)/shard_map/all_to_all | solution.py:72
  101.2 0.2 copy.8
  101.5 0.9 reshape.37
  (3 shorter events, 0.1 us)
Async XLA Ops:
  0.0 7.9 %copy-start = (f32[16,2,4096]{2,1,0:T(2,128)S(1)}, f32[16,2,4096]{2,1,0:T(2,128)}, u32[]{:S(2)}) copy-start(f32[16,2,4096]{2,1,0:T(2,128)} %param.2) | copy-start | bytes 1572868
  1.9 11.6 %collective-permute-start = (f32[16,1,4096]{2,1,0:T(1,128)S(1)}, f32[16,1,4096]{2,1,0:T(1,128)S(1)}, u32[]{:S(2)}, u32[]{:S(2)}) collective-permute-start(f32[16,1,4096]{2,1,0:T(1,128)S(1)} %get-tuple-element.25), channel_id=1, source_target_pairs={{1,0},{2,1},{3,2},{4,3},{5,4},{6,5},{7,6},{0,7},{9,8},{10,9},{11,1... | collective-permute-start | bytes 786440 | tf_op jit(solution)/shard_map/ppermute | solution.py:20
  7.9 10.6 %collective-permute-start.1 = (f32[16,1,4096]{2,1,0:T(1,128)S(1)}, f32[16,1,4096]{2,1,0:T(1,128)}, u32[]{:S(2)}, u32[]{:S(2)}) collective-permute-start(f32[16,1,4096]{2,1,0:T(1,128)S(1)} %get-tuple-element.26), channel_id=1, source_target_pairs={{0,1},{1,2},{2,3},{3,4},{4,5},{5,6},{6,7},{7,0},{8,9},{9,10},{10,1... | collective-permute-start | bytes 786440 | tf_op jit(solution)/shard_map/ppermute | solution.py:17
  9.3 0.8 copy-start.1
  23.9 13.4 %collective-permute-start.2 = (f32[16,1,4096]{2,1,0:T(1,128)}, f32[16,1,4096]{2,1,0:T(1,128)S(1)}, u32[]{:S(2)}, u32[]{:S(2)}) collective-permute-start(f32[16,1,4096]{2,1,0:T(1,128)} %get-tuple-element.23), channel_id=1, source_target_pairs={{1,0},{2,1},{3,2},{4,3},{5,4},{6,5},{7,6},{0,7},{9,8},{10,9},{11,1... | collective-permute-start | bytes 786440 | tf_op jit(solution)/shard_map/ppermute | solution.py:20
  27.3 10.2 %collective-permute-start.3 = (f32[16,1,4096]{2,1,0:T(1,128)}, f32[16,1,4096]{2,1,0:T(1,128)}, u32[]{:S(2)}, u32[]{:S(2)}) collective-permute-start(f32[16,1,4096]{2,1,0:T(1,128)} %get-tuple-element.24), channel_id=1, source_target_pairs={{0,1},{1,2},{2,3},{3,4},{4,5},{5,6},{6,7},{7,0},{8,9},{9,10},{10,1... | collective-permute-start | bytes 786440 | tf_op jit(solution)/shard_map/ppermute | solution.py:17
where the time goes:
time: 103 us; the launch traced here: 102 us
  blocking collectives  56.9 us (55%)
  waiting for transfers between devices  15.7 us (15%)
  starting transfers between devices  9.52 us (9%)
  local copies, waits for them, and re-layouts  9.32 us (9%)
  other arithmetic  7.48 us (7%)
  matrix products  2.54 us (2%)
    psum x1, blocking collectives, local(): gram = lax.psum(partial_value, ('band', 'grid'))  39 us
    ppermute x2, waiting for transfers between devices, with_halo(): lax.ppermute(lax.slice_in_dim(block, 0, width, axis=dim), axis, backward)  10.5 us
    ppermute x2, starting transfers between devices, with_halo(): lax.ppermute(lax.slice_in_dim(block, 0, width, axis=dim), axis, backward)  9.51 us
    all_to_all x1, blocking collectives, local(): lax.all_to_all(turned, 'band', split_axis=0, concat_axis=1, tiled=True)  9.36 us
    all_to_all x1, blocking collectives, local(): lax.all_to_all(filtered, 'band', split_axis=1, concat_axis=0, tiled=True)  8.59 us
    ppermute x2, waiting for transfers between devices, with_halo(): lax.ppermute(lax.slice_in_dim(block, block.shape[dim] - width, None, axis...  5.27 us
    slice x2, local copies, waits for them, and re-layouts, with_halo(): lax.slice_in_dim(block, 0, width, axis=dim)  3.21 us
    convert_element_type x1, other arithmetic, local(): filtered = current.astype(jnp.bfloat16).reshape(count, zplanes * width)  2.58 us
  transfers between devices with their start and end apart: 4, of which 4 were waited for; matrix products, arithmetic and copies ran while one was open for 4% of the time, Pallas kernels for 0%

commit v1 on v0

--- a/solution.py
+++ b/solution.py
@@ -55,7 +55,7 @@
         )
         / total_cells
     )
-    gram = lax.psum(partial_value, ("band", "grid"))
+    gram = lax.psum(lax.psum(partial_value, "band"), "grid")
     scale = jnp.max(jnp.sum(jnp.abs(gram), axis=1))
     identity_mat = jnp.eye(gram.shape[0], dtype=jnp.float32)
     upper = gram / scale

time: 103 us -> 109 us (1.058)
  blocking collectives: 56.9 us -> 63.3 us
    psum x1 -> x2, blocking collectives: 39 us -> 46.3 us  [local(): gram = lax.psum(lax.psum(partial_value, 'band'), 'grid')]
where the time goes in v1:
time: 109 us
  blocking collectives  63.3 us (58%)
  waiting for transfers between devices  15.7 us (14%)
  starting transfers between devices  9.52 us (9%)
  local copies, waits for them, and re-layouts  9.32 us (9%)
  other arithmetic  7.48 us (7%)
  matrix products  2.54 us (2%)
    psum x2, blocking collectives, local(): gram = lax.psum(lax.psum(partial_value, 'band'), 'grid')  46.3 us
    ppermute x2, waiting for transfers between devices, with_halo(): lax.ppermute(lax.slice_in_dim(block, 0, width, axis=dim), axis, backward)  10.5 us
    ppermute x2, starting transfers between devices, with_halo(): lax.ppermute(lax.slice_in_dim(block, 0, width, axis=dim), axis, backward)  9.51 us
    all_to_all x1, blocking collectives, local(): lax.all_to_all(filtered, 'band', split_axis=1, concat_axis=0, tiled=True)  8.59 us
    all_to_all x1, blocking collectives, local(): lax.all_to_all(turned, 'band', split_axis=0, concat_axis=1, tiled=True)  8.39 us
    ppermute x2, waiting for transfers between devices, with_halo(): lax.ppermute(lax.slice_in_dim(block, block.shape[dim] - width, None, axis...  5.27 us
    slice x2, local copies, waits for them, and re-layouts, with_halo(): lax.slice_in_dim(block, 0, width, axis=dim)  3.22 us
    convert_element_type x1, other arithmetic, local(): filtered = current.astype(jnp.bfloat16).reshape(count, zplanes * width)  2.58 us
  transfers between devices with their start and end apart: 4, of which 4 were waited for; matrix products, arithmetic and copies ran while one was open for 4% of the time, Pallas kernels for 0%

profile of v1, /device:TPU:0, one launch (start us, length us, event | category | flops | bytes accessed | tf_op | source)
XLA Modules:
  0.0 108.8 jit_solution(16653641273351321875)
XLA Ops:
  0.0 0.0 copy-start
  0.0 1.9 %fusion.24 = (f32[16,1,4096]{2,1,0:T(1,128)S(1)}, f32[16,1,4096]{2,1,0:T(1,128)S(1)}) fusion(f32[16,2,4096]{2,1,0:T(2,128)} %param.2), kind=kLoop, calls=%fused_computation.42 | loop fusion | bytes 1048576 | tf_op jit(solution)/shard_map/slice | solution.py:20
  1.9 6.1 %collective-permute-start = (f32[16,1,4096]{2,1,0:T(1,128)S(1)}, f32[16,1,4096]{2,1,0:T(1,128)S(1)}, u32[]{:S(2)}, u32[]{:S(2)}) collective-permute-start(f32[16,1,4096]{2,1,0:T(1,128)S(1)} %get-tuple-element.25), channel_id=1, source_target_pairs={{1,0},{2,1},{3,2},{4,3},{5,4},{6,5},{7,6},{0,7},{9,8},{10,9},{11,1... | collective-permute-start | bytes 786440 | tf_op jit(solution)/shard_map/ppermute | solution.py:20
  7.9 0.0 collective-permute-start.1
  7.9 0.0 copy-done
  7.9 0.6 reshape.35
  8.6 0.4 fusion.19
  8.9 0.4 fusion.20
  9.3 0.0 copy-start.1
  9.3 0.2 fusion.21
  9.5 0.5 copy-done.1
  10.1 0.9 fusion.4
  11.0 0.5 add.60
  11.5 2.0 %collective-permute-done = f32[16,1,4096]{2,1,0:T(1,128)S(1)} collective-permute-done((f32[16,1,4096]{2,1,0:T(1,128)S(1)}, f32[16,1,4096]{2,1,0:T(1,128)S(1)}, u32[]{:S(2)}, u32[]{:S(2)}) %collective-permute-start) | collective-permute-done | bytes 262176 | tf_op jit(solution)/shard_map/ppermute | solution.py:20
  13.5 5.0 %collective-permute-done.1 = f32[16,1,4096]{2,1,0:T(1,128)} collective-permute-done((f32[16,1,4096]{2,1,0:T(1,128)S(1)}, f32[16,1,4096]{2,1,0:T(1,128)}, u32[]{:S(2)}, u32[]{:S(2)}) %collective-permute-start.1) | collective-permute-done | bytes 262176 | tf_op jit(solution)/shard_map/ppermute | solution.py:17
  18.5 2.4 %broadcast_multiply_fusion = (f32[16,2,4096]{2,1,0:T(2,128)S(1)}, f32[16,2,4096]{2,1,0:T(2,128)S(1)}) fusion(f32[16,2,4096]{2,1,0:T(2,128)S(1)} %copy-done, f32[2,4096]{1,0:T(2,128)S(1)} %copy-done.1, f32[16,2,4096]{2,1,0:T(2,128)S(1)} %add.60, f32[16,1,4096]{2,1,0:T(1,128)} %collective-permute-done.1, f32[16,1,4096]{2,1,0:T(1,128)S(1)} %collective-permute-done), kind=kLoop, calls=%fused_computation.26 | loop fusion | flops 1572864 | bytes 2654208 | tf_op jit(solution)/shard_map/div | solution.py:43
  21.0 0.6 reshape.36
  21.6 0.4 fusion.16
  22.0 0.2 fusion.17
  22.2 0.4 fusion.15
  22.5 1.3 %fusion.23 = (f32[16,1,4096]{2,1,0:T(1,128)}, f32[16,1,4096]{2,1,0:T(1,128)}) fusion(f32[16,2,4096]{2,1,0:T(2,128)S(1)} %get-tuple-element.5), kind=kLoop, calls=%fused_computation.41 | loop fusion | bytes 1048576 | tf_op jit(solution)/shard_map/slice | solution.py:20
  23.9 3.5 %collective-permute-start.2 = (f32[16,1,4096]{2,1,0:T(1,128)}, f32[16,1,4096]{2,1,0:T(1,128)S(1)}, u32[]{:S(2)}, u32[]{:S(2)}) collective-permute-start(f32[16,1,4096]{2,1,0:T(1,128)} %get-tuple-element.23), channel_id=1, source_target_pairs={{1,0},{2,1},{3,2},{4,3},{5,4},{6,5},{7,6},{0,7},{9,8},{10,9},{11,1... | collective-permute-start | bytes 786440 | tf_op jit(solution)/shard_map/ppermute | solution.py:20
  27.3 0.0 collective-permute-start.3
  27.4 0.9 fusion.6
  28.2 0.5 add.67
  28.8 8.5 %collective-permute-done.2 = f32[16,1,4096]{2,1,0:T(1,128)S(1)} collective-permute-done((f32[16,1,4096]{2,1,0:T(1,128)}, f32[16,1,4096]{2,1,0:T(1,128)S(1)}, u32[]{:S(2)}, u32[]{:S(2)}) %collective-permute-start.2) | collective-permute-done | bytes 262176 | tf_op jit(solution)/shard_map/ppermute | solution.py:20
  37.3 0.3 collective-permute-done.3
  37.5 2.6 %subtract_convert_fusion = bf16[16,2,4096]{2,1,0:T(2,128)(2,1)S(1)} fusion(f32[16,2,4096]{2,1,0:T(2,128)S(1)} %copy-done, f32[16,2,4096]{2,1,0:T(2,128)S(1)} %get-tuple-element.6, f32[16,2,4096]{2,1,0:T(2,128)S(1)} %add.67, f32[16,2,4096]{2,1,0:T(2,128)S(1)} %get-tuple-element.5, f32[16,1,4096]{2,1,0:T(1,128)} %collective-permute-done.3, ...), kind=kLoop, calls=%fused_computation.24 | loop fusion | flops 1835008 | bytes 2916352 | tf_op jit(solution)/shard_map/convert_element_type | solution.py:49
  40.1 0.1 all_to_all.26
  40.2 0.2 copy.7
  40.3 8.6 %all_to_all.35 = bf16[16,4,2048]{2,0,1:T(8,128)(2,1)S(1)} all-to-all(bf16[16,4,2048]{2,0,1:T(8,128)(2,1)S(1)} %copy.7), channel_id=1, replica_groups=mesh['band'=4,'grid'=8] {'band'}, dimensions={1} | all-to-all | bytes 524288 | tf_op jit(solution)/shard_map/all_to_all | solution.py:50
  48.9 0.2 convolution_multiply_fusion.2
  49.1 10.3 %psum.14 = f32[64,64]{1,0:T(8,128)S(1)} all-reduce(f32[64,64]{1,0:T(8,128)S(1)} %convolution_multiply_fusion.2), channel_id=1, replica_groups=mesh['band'=4,'grid'=8] {'band'}, use_global_device_ids=true, to_apply=%region_0.1 | all-reduce | flops 4096 | bytes 32768 | tf_op jit(solution)/shard_map/psum | solution.py:58
  59.4 36.1 %psum.15 = f32[64,64]{1,0:T(8,128)S(1)} all-reduce(f32[64,64]{1,0:T(8,128)S(1)} %psum.14), channel_id=1, replica_groups=mesh['band'=4,'grid'=8] {'grid'}, use_global_device_ids=true, to_apply=%region_1.2 | all-reduce | flops 4096 | bytes 32768 | tf_op jit(solution)/shard_map/psum | solution.py:58
  95.5 0.1 abs_reduce_fusion
  95.6 0.6 reduce_max.9
  96.2 0.8 fusion.1
  97.0 0.8 fusion.14
  97.8 0.1 fusion.13
  98.7 0.2 fusion
  98.8 0.2 fusion.2
  99.0 0.2 convolution_convert_fusion
  99.3 8.4 %all_to_all.36 = bf16[4,16,2048]{2,1,0:T(8,128)(2,1)S(1)} all-to-all(bf16[4,16,2048]{2,1,0:T(8,128)(2,1)S(1)} %bitcast.21), channel_id=1, replica_groups=mesh['band'=4,'grid'=8] {'band'}, dimensions={0} | all-to-all | bytes 524288 | tf_op jit(solution)/shard_map/all_to_all | solution.py:72
  107.7 0.2 copy.8
  107.9 0.9 reshape.37
  (3 shorter events, 0.1 us)
Async XLA Ops:
  0.0 7.9 %copy-start = (f32[16,2,4096]{2,1,0:T(2,128)S(1)}, f32[16,2,4096]{2,1,0:T(2,128)}, u32[]{:S(2)}) copy-start(f32[16,2,4096]{2,1,0:T(2,128)} %param.2) | copy-start | bytes 1572868
  1.9 11.6 %collective-permute-start = (f32[16,1,4096]{2,1,0:T(1,128)S(1)}, f32[16,1,4096]{2,1,0:T(1,128)S(1)}, u32[]{:S(2)}, u32[]{:S(2)}) collective-permute-start(f32[16,1,4096]{2,1,0:T(1,128)S(1)} %get-tuple-element.25), channel_id=1, source_target_pairs={{1,0},{2,1},{3,2},{4,3},{5,4},{6,5},{7,6},{0,7},{9,8},{10,9},{11,1... | collective-permute-start | bytes 786440 | tf_op jit(solution)/shard_map/ppermute | solution.py:20
  7.9 10.6 %collective-permute-start.1 = (f32[16,1,4096]{2,1,0:T(1,128)S(1)}, f32[16,1,4096]{2,1,0:T(1,128)}, u32[]{:S(2)}, u32[]{:S(2)}) collective-permute-start(f32[16,1,4096]{2,1,0:T(1,128)S(1)} %get-tuple-element.26), channel_id=1, source_target_pairs={{0,1},{1,2},{2,3},{3,4},{4,5},{5,6},{6,7},{7,0},{8,9},{9,10},{10,1... | collective-permute-start | bytes 786440 | tf_op jit(solution)/shard_map/ppermute | solution.py:17
  9.3 0.8 copy-start.1
  23.9 13.4 %collective-permute-start.2 = (f32[16,1,4096]{2,1,0:T(1,128)}, f32[16,1,4096]{2,1,0:T(1,128)S(1)}, u32[]{:S(2)}, u32[]{:S(2)}) collective-permute-start(f32[16,1,4096]{2,1,0:T(1,128)} %get-tuple-element.23), channel_id=1, source_target_pairs={{1,0},{2,1},{3,2},{4,3},{5,4},{6,5},{7,6},{0,7},{9,8},{10,9},{11,1... | collective-permute-start | bytes 786440 | tf_op jit(solution)/shard_map/ppermute | solution.py:20
  27.3 10.2 %collective-permute-start.3 = (f32[16,1,4096]{2,1,0:T(1,128)}, f32[16,1,4096]{2,1,0:T(1,128)}, u32[]{:S(2)}, u32[]{:S(2)}) collective-permute-start(f32[16,1,4096]{2,1,0:T(1,128)} %get-tuple-element.24), channel_id=1, source_target_pairs={{0,1},{1,2},{2,3},{3,4},{4,5},{5,6},{6,7},{7,0},{8,9},{9,10},{10,1... | collective-permute-start | bytes 786440 | tf_op jit(solution)/shard_map/ppermute | solution.py:17
